TPU v7x, 128 devices: a whole 4x4x4 slice. The times are simulated.
128 devices in a mesh: cluster: 8 (over x, core), row: 16 (over z, y).
Axes of the slice: x: 4, y: 4, z: 4, core: 2. Of those that a mesh axis runs over, the one named last changes fastest.
Arguments:
- sources: bfloat16 [32768, 512], P(('cluster', 'row')), may hold values from -12 to 12
- targets: bfloat16 [32768, 512], P(('cluster', 'row')), may hold values from -12 to 12
- source_order: int32 [32768], P(('cluster', 'row')), may hold values from 0 to 255, as said below
- target_order: int32 [32768], P(('cluster', 'row')), may hold values from 0 to 255, as said below
Outputs:
- source_map: bfloat16 [32768, 512], P(('cluster', 'row'))
- target_map: bfloat16 [32768, 512], P(('cluster', 'row'))
Inputs may be any that keep to these rules, and one draw needn't show every extreme that they name: `source_order`: in each aligned block of 256 consecutive rows every value appears exactly once, so each block holds 32 source rows of every co-cluster. `target_order`: in each aligned block of 256 consecutive rows every value appears exactly once, so each block holds 32 target rows of every co-cluster.
All inputs are finite; a program needn't handle non-finite values.
Results may differ from a plain program's by a relative error of at most 0.01.
Values may be sent and summed in bfloat16 or wider, within the bound.
No kernel may reach another device: no remote copies, remote signals or barrier semaphores. Data moves between devices by JAX's collectives and lax.ppermute only.
A program may use at most 64 MiB of HBM per device.

v0:
```python
import math
import jax
import jax.numpy as jnp
from jax import lax
from jax.sharding import PartitionSpec as P

ITERS = 3
entropy_weight = 0.02


def square_sums(matrix):
    widened = matrix.astype(jnp.float32)
    return jnp.sum(widened * widened, axis=1)


def cost_panel(source_rows, source_norms, target_rows, target_norms):
    inner = jnp.einsum("id,jd->ij", source_rows, target_rows, preferred_element_type=jnp.float32)
    return (source_norms[:, None] + target_norms[None, :] - 2.0 * inner) / source_rows.shape[1]


def into_slots(ordering, matrix):
    positions = jnp.arange(matrix.shape[0], dtype=jnp.int32)
    selector = (positions[:, None] == ordering[None, :]).astype(jnp.bfloat16)
    return jnp.dot(selector, matrix, preferred_element_type=jnp.float32).astype(jnp.bfloat16)


def out_of_slots(ordering, matrix):
    positions = jnp.arange(matrix.shape[0], dtype=jnp.int32)
    selector = (ordering[:, None] == positions[None, :]).astype(jnp.bfloat16)
    return jnp.dot(selector, matrix, preferred_element_type=jnp.float32).astype(jnp.bfloat16)


def shards(sources, targets, source_order, target_order):
    rows_dev = sources.shape[0]
    width = sources.shape[1]
    sent_sources = into_slots(source_order, sources)
    sent_targets = into_slots(target_order, targets)
    local_sources, local_targets = (
        lax.all_to_all(sent_sources, "cluster", split_axis=0, concat_axis=0, tiled=True),
        lax.all_to_all(sent_targets, "cluster", split_axis=0, concat_axis=0, tiled=True),
    )
    cluster_targets = lax.all_gather(local_targets, "row", axis=0, tiled=True)
    columns = cluster_targets.shape[0]
    span = 512
    pieces = columns // span
    target_norms = square_sums(cluster_targets)
    target_blocks = cluster_targets.reshape(pieces, span, width)
    norm_blocks = target_norms.reshape(pieces, span)
    source_norms = square_sums(local_sources)
    log_mass = -math.log(columns)

    def row_lse(potential):

        def row_advance(carry, item):
            running, totals = carry
            block, block_norms, block_potential = item
            scores = (
                block_potential[None, :]
                - cost_panel(local_sources, source_norms, block, block_norms)
            ) / entropy_weight
            highest = jnp.maximum(running, jnp.max(scores, axis=1))
            totals = totals * jnp.exp(running - highest) + jnp.sum(
                jnp.exp(scores - highest[:, None]), axis=1
            )
            return ((highest, totals), None)

        start = (jnp.full((rows_dev,), -jnp.inf, jnp.float32), jnp.zeros((rows_dev,), jnp.float32))
        (running, totals), unused = lax.scan(
            row_advance, start, (target_blocks, norm_blocks, potential.reshape(pieces, span))
        )
        return running + jnp.log(totals)

    def column_lse(source_potential):

        def column_advance(carry, item):
            block, block_norms = item
            scores = (
                source_potential[:, None]
                - cost_panel(local_sources, source_norms, block, block_norms)
            ) / entropy_weight
            highest = jnp.max(scores, axis=0)
            return (carry, (highest, jnp.sum(jnp.exp(scores - highest[None, :]), axis=0)))

        unused, (peaks, totals) = lax.scan(column_advance, 0, (target_blocks, norm_blocks))
        peaks = peaks.reshape(-1)
        totals = totals.reshape(-1)
        highest = lax.pmax(peaks, "row")
        summed = lax.psum(totals * jnp.exp(peaks - highest), "row")
        return highest + jnp.log(summed)

    target_potential = jnp.zeros((columns,), jnp.float32)
    for repeat in range(ITERS):
        source_potential = entropy_weight * (log_mass - row_lse(target_potential))
        column_norm = column_lse(source_potential)
        target_potential = entropy_weight * (log_mass - column_norm)
    block = cluster_targets
    block_norms = target_norms
    scores = (
        source_potential[:, None] - cost_panel(local_sources, source_norms, block, block_norms)
    ) / entropy_weight
    weights = jnp.exp(scores - column_norm[None, :]).astype(jnp.bfloat16)
    target_map = lax.psum_scatter(
        jnp.einsum("ij,id->jd", weights, local_sources, preferred_element_type=jnp.float32).astype(
            jnp.bfloat16
        ),
        "row",
        scatter_dimension=0,
        tiled=True,
    )
    row_norm = row_lse(target_potential)

    def accumulate(carry, item):
        block, block_norms, block_potential = item
        scores = (
            block_potential[None, :] - cost_panel(local_sources, source_norms, block, block_norms)
        ) / entropy_weight
        weights = jnp.exp(scores - row_norm[:, None]).astype(jnp.bfloat16)
        return (carry + jnp.dot(weights, block, preferred_element_type=jnp.float32), None)

    source_sums, unused = lax.scan(
        accumulate,
        jnp.zeros((rows_dev, width), jnp.float32),
        (target_blocks, norm_blocks, target_potential.reshape(pieces, span)),
    )
    source_map = source_sums.astype(jnp.bfloat16)
    back_sources, back_targets = (
        lax.all_to_all(source_map, "cluster", split_axis=0, concat_axis=0, tiled=True),
        lax.all_to_all(target_map, "cluster", split_axis=0, concat_axis=0, tiled=True),
    )
    return (out_of_slots(source_order, back_sources), out_of_slots(target_order, back_targets))


def solution(mesh):
    return jax.shard_map(
        shards,
        mesh=mesh,
        in_specs=(
            P(("cluster", "row"), None),
            P(("cluster", "row"), None),
            P(("cluster", "row")),
            P(("cluster", "row")),
        ),
        out_specs=(P(("cluster", "row"), None), P(("cluster", "row"), None)),
        check_vma=False,
    )
```

profile of v0, /device:TPU:1, one launch (start us, length us, event | category | flops | bytes accessed | tf_op | source)
XLA Modules:
  0.0 678.2 jit_solution(1268138748987792291)
XLA Ops:
  9.0 12.2 %all_to_all.48 = bf16[8,32,512]{2,1,0:T(8,128)(2,1)} all-to-all(bf16[8,32,512]{2,1,0:T(8,128)(2,1)S(1)} %bitcast.260), channel_id=1, replica_groups=mesh['cluster'=8,'row'=16] {'cluster'}, dimensions={0} | all-to-all | bytes 524288 | tf_op jit(solution)/shard_map/all_to_all | solution.py:40
  23.1 4.4 all-to-all-start
  27.6 6.4 all-to-all-done
  34.2 39.4 %all-gather.2.cloned.1.call-done = bf16[4096,512]{1,0:T(8,128)(2,1)} async-done(((bf16[256,512]{1,0:T(8,128)(2,1)}), bf16[4096,512]{1,0:T(8,128)(2,1)}) %all-gather.2.cloned.1.call-update) | async-done | bytes 4194320 | tf_op jit(solution)/shard_map/all_gather | solution.py:42
  73.6 3.1 multiply_reduce_fusion
  76.7 12.7 %while.102 = (s32[]{:T(128)}, f32[256]{0:T(256)S(1)}, f32[256]{0:T(256)S(1)}, f32[256]{0:T(256)S(1)}, f32[8,512]{1,0:T(8,128)S(1)}, /*index=5*/bf16[8,512,512]{2...) while((s32[]{:T(128)}, f32[256]{0:T(256)S(1)}, f32[256]{0:T(256)S(1)}, ...), condition=%wide.region_5.6_spmd.clone, body=%wide.region_2.5_spmd.clone.sunk | while | flops 135398656 | bytes 1856108 | solution.py:68
  89.5 13.7 %while.99 = (s32[]{:T(128)}, f32[8,512]{1,0:T(8,128)S(1)}, f32[8,512]{1,0:T(8,128)S(1)}, f32[256]{0:T(256)S(1)}, f32[256]{0:T(256)S(1)}, /*index=5*/f32[8,512]{1...) while((s32[]{:T(128)}, f32[8,512]{1,0:T(8,128)S(1)}, ...), condition=%wide.region_9.10_spmd, body=%wide.region_6.9_spmd.sunk | while | flops 135396352 | bytes 1858161 | solution.py:84
  103.2 58.3 %pmax.21 = f32[4096]{0:T(1024)S(1)} all-reduce(f32[4096]{0:T(1024)S(1)} %bitcast.268), channel_id=1, replica_groups=mesh['cluster'=8,'row'=16] {'row'}, use_global_device_ids=true, to_apply=%region_10.11 | all-reduce | flops 4096 | bytes 32768 | tf_op jit(solution)/shard_map/pmax | solution.py:87
  161.5 55.6 %psum.21 = f32[4096]{0:T(1024)S(1)} all-reduce(f32[4096]{0:T(1024)S(1)} %exponential_multiply_fusion.2), channel_id=1, replica_groups=mesh['cluster'=8,'row'=16] {'row'}, use_global_device_ids=true, to_apply=%region_11.12 | all-reduce | flops 4096 | bytes 32768 | tf_op jit(solution)/shard_map/psum | solution.py:88
  217.1 12.8 %while.103 = (s32[]{:T(128)}, f32[256]{0:T(256)S(1)}, f32[256]{0:T(256)S(1)}, f32[8,512]{1,0:T(8,128)S(1)}, f32[256]{0:T(256)S(1)}, /*index=5*/f32[8,512]{1,0:T(...) while((s32[]{:T(128)}, f32[256]{0:T(256)S(1)}, ...), condition=%wide.region_15.16_spmd.clone, body=%wide.region_12.15_spmd.clone.sunk | while | flops 135398656 | bytes 1862260 | solution.py:68
  230.0 13.7 %while.100 = (s32[]{:T(128)}, f32[8,512]{1,0:T(8,128)S(1)}, f32[8,512]{1,0:T(8,128)S(1)}, f32[256]{0:T(256)S(1)}, f32[256]{0:T(256)S(1)}, /*index=5*/f32[8,512]{...) while((s32[]{:T(128)}, f32[8,512]{1,0:T(8,128)S(1)}, ...), condition=%wide.region_19.20_spmd, body=%wide.region_16.19_spmd.sunk | while | flops 135396352 | bytes 1858161 | solution.py:84
  243.7 55.6 %pmax.22 = f32[4096]{0:T(1024)S(1)} all-reduce(f32[4096]{0:T(1024)S(1)} %bitcast.270), channel_id=1, replica_groups=mesh['cluster'=8,'row'=16] {'row'}, use_global_device_ids=true, to_apply=%region_20.21 | all-reduce | flops 4096 | bytes 32768 | tf_op jit(solution)/shard_map/pmax | solution.py:87
  299.4 56.0 %psum.22 = f32[4096]{0:T(1024)S(1)} all-reduce(f32[4096]{0:T(1024)S(1)} %exponential_multiply_fusion.1), channel_id=1, replica_groups=mesh['cluster'=8,'row'=16] {'row'}, use_global_device_ids=true, to_apply=%region_21.22 | all-reduce | flops 4096 | bytes 32768 | tf_op jit(solution)/shard_map/psum | solution.py:88
  355.3 12.8 %while.104 = (s32[]{:T(128)}, f32[256]{0:T(256)S(1)}, f32[256]{0:T(256)S(1)}, f32[8,512]{1,0:T(8,128)S(1)}, f32[256]{0:T(256)S(1)}, /*index=5*/f32[8,512]{1,0:T(...) while((s32[]{:T(128)}, f32[256]{0:T(256)S(1)}, ...), condition=%wide.region_25.26_spmd.clone, body=%wide.region_22.25_spmd.clone.sunk | while | flops 135398656 | bytes 1862260 | solution.py:68
  368.2 13.7 %while.101 = (s32[]{:T(128)}, f32[8,512]{1,0:T(8,128)S(1)}, f32[8,512]{1,0:T(8,128)S(1)}, f32[256]{0:T(256)S(1)}, f32[256]{0:T(256)S(1)}, /*index=5*/f32[8,512]{...) while((s32[]{:T(128)}, f32[8,512]{1,0:T(8,128)S(1)}, ...), condition=%wide.region_29.30_spmd, body=%wide.region_26.29_spmd.sunk | while | flops 135396352 | bytes 1858161 | solution.py:84
  382.0 55.6 %pmax.23 = f32[4096]{0:T(1024)S(1)} all-reduce(f32[4096]{0:T(1024)S(1)} %bitcast.272), channel_id=1, replica_groups=mesh['cluster'=8,'row'=16] {'row'}, use_global_device_ids=true, to_apply=%region_30.31 | all-reduce | flops 4096 | bytes 32768 | tf_op jit(solution)/shard_map/pmax | solution.py:87
  437.6 55.6 %psum.23 = f32[4096]{0:T(1024)S(1)} all-reduce(f32[4096]{0:T(1024)S(1)} %exponential_multiply_fusion), channel_id=1, replica_groups=mesh['cluster'=8,'row'=16] {'row'}, use_global_device_ids=true, to_apply=%region_31.32 | all-reduce | flops 4096 | bytes 32768 | tf_op jit(solution)/shard_map/psum | solution.py:88
  493.2 7.0 %convolution_convert_fusion = bf16[4096,512]{1,0:T(8,128)(2,1)} fusion(bf16[256,512]{1,0:T(8,128)(2,1)S(1)} %get-tuple-element.1322, bf16[4096,512]{1,0:T(8,128)(2,1)} %bitcast.254, f32[4096]{0:T(1024)S(1)} %get-tuple-element.614, f32[4096]{0:T(1024)S(1)} %multiply_reduce_fusion, f32[256]{0:T(256)S(1)} %get-tuple-element.1343, f32[256]{0:T(256)S(1)} %get-tuple-element.1345), kind=kOutput, calls=%fused_computation.123 | convolution fusion | flops 2157969408 | bytes 8685568 | tf_op jit(solution)/shard_map/ij,id->jd/dot_general | solution.py:103
  500.2 12.8 %while.105 = (s32[]{:T(128)}, f32[256]{0:T(256)S(1)}, f32[256]{0:T(256)S(1)}, f32[8,512]{1,0:T(8,128)S(1)}, f32[256]{0:T(256)S(1)}, /*index=5*/f32[8,512]{1,0:T(...) while((s32[]{:T(128)}, f32[256]{0:T(256)S(1)}, ...), condition=%wide.region_35.36_spmd.clone, body=%wide.region_32.35_spmd.clone.sunk | while | flops 135398656 | bytes 1862260 | solution.py:68
  513.1 15.4 %while.106 = (s32[]{:T(128)}, f32[256,512]{1,0:T(8,128)S(1)}, f32[8,512]{1,0:T(8,128)S(1)}, f32[256]{0:T(256)S(1)}, f32[8,512]{1,0:T(8,128)S(1)}, /*index=5*/bf1...) while((s32[]{:T(128)}, f32[256,512]{1,0:T(8,128)S(1)}, ...), condition=%wide.region_37.38_spmd.clone, body=%wide.region_36.37_spmd.clone.sunk | while | flops 269746176 | bytes 2374771 | solution.py:120
  528.5 94.9 %all_to_all.49 = bf16[8,32,512]{2,1,0:T(8,128)(2,1)S(1)} all-to-all(bf16[8,32,512]{2,1,0:T(8,128)(2,1)S(1)} %bitcast.255), channel_id=1, replica_groups=mesh['cluster'=8,'row'=16] {'cluster'}, dimensions={0} | all-to-all | bytes 524288 | tf_op jit(solution)/shard_map/all_to_all | solution.py:127
  623.4 33.8 %reduce-scatter.2.cloned.1.call-done = bf16[256,512]{1,0:T(8,128)(2,1)} async-done(((bf16[4096,512]{1,0:T(8,128)(2,1)}), bf16[256,512]{1,0:T(8,128)(2,1)}) %reduce-scatter.2.cloned.1.call-update) | async-done | bytes 262160 | tf_op jit(solution)/shard_map/reduce_scatter | solution.py:102
  657.2 6.7 all-to-all-start.3
  664.9 5.5 all-to-all-done.3
  (380 shorter events, 111.3 us)
Async XLA Ops:
  7.2 1.0 copy-start
  7.2 66.4 %all-gather.2.cloned.1.call-start = ((), (), s32[]{:S(2)}) async-start(), calls=%async_computation.5 | async-start | bytes 4456448 | tf_op jit(solution)/shard_map/all_gather | solution.py:42
  23.1 10.8 %all-to-all-start = ((bf16[8,32,512]{2,1,0:T(8,128)(2,1)}), bf16[8,32,512]{2,1,0:T(8,128)(2,1)S(1)}, u32[]{:S(2)}, u32[]{:S(2)}) async-start(bf16[8,32,512]{2,1,0:T(8,128)(2,1)} %bitcast.15), calls=%async_computation | async-start | bytes 524288 | tf_op jit(solution)/shard_map/all_to_all | solution.py:39
  27.5 629.7 %reduce-scatter.2.cloned.1.call-start = ((), (), s32[]{:S(2)}) async-start(), calls=%async_computation.6 | async-start | bytes 4456448 | tf_op jit(solution)/shard_map/reduce_scatter | solution.py:102
  513.1 150.8 %copy-start.1 = (s32[256]{0:T(256)S(1)}, s32[256]{0:T(256)}, u32[]{:S(2)}) copy-start(s32[256]{0:T(256)} %param.22) | copy-start | bytes 3076
  513.1 157.3 %copy-start.2 = (s32[256]{0:T(256)S(1)}, s32[256]{0:T(256)}, u32[]{:S(2)}) copy-start(s32[256]{0:T(256)} %param.23) | copy-start | bytes 3076
  657.2 13.2 %all-to-all-start.3 = ((bf16[8,32,512]{2,1,0:T(8,128)(2,1)}), bf16[8,32,512]{2,1,0:T(8,128)(2,1)S(1)}, u32[]{:S(2)}, u32[]{:S(2)}) async-start(bf16[8,32,512]{2,1,0:T(8,128)(2,1)} %bitcast.261), calls=%async_computation.4 | async-start | bytes 524288 | tf_op jit(solution)/shard_map/all_to_all | solution.py:128
Sparse Core Ops, SparseCore 0:
  21.3 52.2 all-gather.1
  500.3 156.7 reduce-scatter.1
where the time goes:
time: 682 us; the launch traced here: 678 us
  blocking collectives  444 us (65%)
  matrix products  106 us (16%)
  waiting for transfers between devices  85.2 us (12%)
  between operations  14.3 us (2%)
  starting transfers between devices  11.1 us (2%)
  other arithmetic  10.7 us (2%)
    pmax x3, blocking collectives, column_lse(): highest = lax.pmax(peaks, 'row')  170 us
    psum x3, blocking collectives, column_lse(): summed = lax.psum(totals * jnp.exp(peaks - highest), 'row')  167 us
    all_to_all x1, blocking collectives, shards(): lax.all_to_all(source_map, 'cluster', split_axis=0, concat_axis=0, tiled=...  94.9 us
    dot_general x56, matrix products, cost_panel(): jnp.einsum('id,jd->ij', source_rows, target_rows, preferred_element_type=...  79.3 us
    all_gather x1, waiting for transfers between devices, shards(): cluster_targets = lax.all_gather(local_targets, 'row', axis=0, tiled=True)  39.4 us
    reduce_scatter x1, waiting for transfers between devices, shards(): lax.psum_scatter(jnp.einsum('ij,id->jd', weights, local_sources, preferre...  33.8 us
    dot_general x8, matrix products, accumulate(): jnp.dot(weights, block, preferred_element_type=jnp.float32)  15 us
  transfers between devices with their start and end apart: 4, of which 4 were waited for; matrix products, arithmetic and copies ran while one was open for 5% of the time, Pallas kernels for 0%

commit v1 on v0

--- a/solution.py
+++ b/solution.py
@@ -1,3 +1,4 @@
+import functools
 import math
 import jax
 import jax.numpy as jnp
@@ -6,6 +7,16 @@
 
 ITERS = 3
 entropy_weight = 0.02
+
+
+def _state_files(field_in, dimension_no):
+    reply = jnp.concatenate(
+        lax.all_to_all(jnp.stack([field_in] * lax.axis_size("row")), "row", 0, 0), axis=dimension_no
+    )
+    return reply
+
+
+types_trace = functools.partial(_state_files, dimension_no=0)
 
 
 def square_sums(matrix):
@@ -39,7 +50,7 @@
         lax.all_to_all(sent_sources, "cluster", split_axis=0, concat_axis=0, tiled=True),
         lax.all_to_all(sent_targets, "cluster", split_axis=0, concat_axis=0, tiled=True),
     )
-    cluster_targets = lax.all_gather(local_targets, "row", axis=0, tiled=True)
+    cluster_targets = types_trace(local_targets)
     columns = cluster_targets.shape[0]
     span = 512
     pieces = columns // span

time: 682 us -> 711 us (1.043)
  waiting for transfers between devices: 85.2 us -> 106 us
  starting transfers between devices: 11.1 us -> 20.4 us
    all_to_all x1 -> x2, waiting for transfers between devices: 6.43 us -> 66.5 us  [the longest x1 61.2 us: _state_files(): lax.all_to_all(jnp.stack([field_in] * lax.axis_size('row')), 'row', 0, 0)]
    all_gather x1 -> x0, waiting for transfers between devices: 39.4 us -> none  [shards(): cluster_targets = lax.all_gather(local_targets, 'row', axis=0, tiled=True)]
    all_to_all x1 -> x2, starting transfers between devices: 4.35 us -> 13.6 us  [the longest x1 7.82 us: _state_files(): lax.all_to_all(jnp.stack([field_in] * lax.axis_size('row')), 'row', 0, 0)]
  transfers between devices with their start and end apart: 4 -> 4, of which waited for: 4 -> 4; matrix products, arithmetic and copies ran while one was open for 5% -> 4% of each run, Pallas kernels for 0% -> 0%
where the time goes in v1:
time: 711 us; the launch traced here: 707 us
  blocking collectives  440 us (62%)
  matrix products  106 us (15%)
  waiting for transfers between devices  106 us (15%)
  starting transfers between devices  20.4 us (3%)
  between operations  14.4 us (2%)
  other arithmetic  10.7 us (2%)
    pmax x3, blocking collectives, column_lse(): highest = lax.pmax(peaks, 'row')  169 us
    psum x3, blocking collectives, column_lse(): summed = lax.psum(totals * jnp.exp(peaks - highest), 'row')  168 us
    all_to_all x1, blocking collectives, shards(): lax.all_to_all(source_map, 'cluster', split_axis=0, concat_axis=0, tiled=...  93.7 us
    dot_general x56, matrix products, cost_panel(): jnp.einsum('id,jd->ij', source_rows, target_rows, preferred_element_type=...  79.4 us
    all_to_all x1, waiting for transfers between devices, _state_files(): lax.all_to_all(jnp.stack([field_in] * lax.axis_size('row')), 'row', 0, 0)  61.2 us
    reduce_scatter x1, waiting for transfers between devices, shards(): lax.psum_scatter(jnp.einsum('ij,id->jd', weights, local_sources, preferre...  33.7 us
    dot_general x8, matrix products, accumulate(): jnp.dot(weights, block, preferred_element_type=jnp.float32)  15 us
  transfers between devices with their start and end apart: 4, of which 4 were waited for; matrix products, arithmetic and copies ran while one was open for 4% of the time, Pallas kernels for 0%

profile of v1, /device:TPU:1, one launch (start us, length us, event | category | flops | bytes accessed | tf_op | source)
XLA Modules:
  0.0 707.3 jit_solution(3248353970272856492)
XLA Ops:
  9.7 5.8 all-to-all-start.1
  16.7 5.3 all-to-all-done.1
  22.0 9.9 %all_to_all.50 = bf16[8,32,512]{2,1,0:T(8,128)(2,1)S(1)} all-to-all(bf16[8,32,512]{2,1,0:T(8,128)(2,1)S(1)} %bitcast.261), channel_id=1, replica_groups=mesh['cluster'=8,'row'=16] {'cluster'}, dimensions={0} | all-to-all | bytes 524288 | tf_op jit(solution)/shard_map/all_to_all | solution.py:50
  34.3 7.8 %all-to-all-start.2 = ((bf16[16,256,512]{2,1,0:T(8,128)(2,1)}), bf16[16,256,512]{2,1,0:T(8,128)(2,1)}, u32[]{:S(2)}, u32[]{:S(2)}) async-start(bf16[16,256,512]{2,1,0:T(8,128)(2,1)} %stack.5), calls=%async_computation.2 | async-start | bytes 8388608 | tf_op jit(solution)/shard_map/all_to_all | solution.py:14
  42.4 61.2 %all-to-all-done.2 = bf16[16,256,512]{2,1,0:T(8,128)(2,1)} async-done(((bf16[16,256,512]{2,1,0:T(8,128)(2,1)}), bf16[16,256,512]{2,1,0:T(8,128)(2,1)}, u32[]{:S(2)}, u32[]{:S(2)}) %all-to-all-start.2) | async-done | bytes 4194336 | tf_op jit(solution)/shard_map/all_to_all | solution.py:14
  106.8 12.7 %while.102 = (s32[]{:T(128)}, f32[256]{0:T(256)S(1)}, f32[256]{0:T(256)S(1)}, f32[256]{0:T(256)S(1)}, f32[8,512]{1,0:T(8,128)S(1)}, /*index=5*/bf16[8,512,512]{2...) while((s32[]{:T(128)}, f32[256]{0:T(256)S(1)}, f32[256]{0:T(256)S(1)}, ...), condition=%wide.region_5.6_spmd.clone, body=%wide.region_2.5_spmd.clone.sunk | while | flops 135398656 | bytes 1856108 | solution.py:79
  119.5 13.7 %while.99 = (s32[]{:T(128)}, f32[8,512]{1,0:T(8,128)S(1)}, f32[8,512]{1,0:T(8,128)S(1)}, f32[256]{0:T(256)S(1)}, f32[256]{0:T(256)S(1)}, /*index=5*/f32[8,512]{1...) while((s32[]{:T(128)}, f32[8,512]{1,0:T(8,128)S(1)}, ...), condition=%wide.region_9.10_spmd, body=%wide.region_6.9_spmd.sunk | while | flops 135396352 | bytes 1858161 | solution.py:95
  133.3 57.7 %pmax.21 = f32[4096]{0:T(1024)S(1)} all-reduce(f32[4096]{0:T(1024)S(1)} %bitcast.270), channel_id=1, replica_groups=mesh['cluster'=8,'row'=16] {'row'}, use_global_device_ids=true, to_apply=%region_10.11 | all-reduce | flops 4096 | bytes 32768 | tf_op jit(solution)/shard_map/pmax | solution.py:98
  191.0 55.9 %psum.21 = f32[4096]{0:T(1024)S(1)} all-reduce(f32[4096]{0:T(1024)S(1)} %exponential_multiply_fusion.2), channel_id=1, replica_groups=mesh['cluster'=8,'row'=16] {'row'}, use_global_device_ids=true, to_apply=%region_11.12 | all-reduce | flops 4096 | bytes 32768 | tf_op jit(solution)/shard_map/psum | solution.py:99
  247.0 12.8 %while.103 = (s32[]{:T(128)}, f32[256]{0:T(256)S(1)}, f32[256]{0:T(256)S(1)}, f32[8,512]{1,0:T(8,128)S(1)}, f32[256]{0:T(256)S(1)}, /*index=5*/f32[8,512]{1,0:T(...) while((s32[]{:T(128)}, f32[256]{0:T(256)S(1)}, ...), condition=%wide.region_15.16_spmd.clone, body=%wide.region_12.15_spmd.clone.sunk | while | flops 135398656 | bytes 1862260 | solution.py:79
  259.9 13.7 %while.100 = (s32[]{:T(128)}, f32[8,512]{1,0:T(8,128)S(1)}, f32[8,512]{1,0:T(8,128)S(1)}, f32[256]{0:T(256)S(1)}, f32[256]{0:T(256)S(1)}, /*index=5*/f32[8,512]{...) while((s32[]{:T(128)}, f32[8,512]{1,0:T(8,128)S(1)}, ...), condition=%wide.region_19.20_spmd, body=%wide.region_16.19_spmd.sunk | while | flops 135396352 | bytes 1858161 | solution.py:95
  273.6 55.8 %pmax.22 = f32[4096]{0:T(1024)S(1)} all-reduce(f32[4096]{0:T(1024)S(1)} %bitcast.272), channel_id=1, replica_groups=mesh['cluster'=8,'row'=16] {'row'}, use_global_device_ids=true, to_apply=%region_20.21 | all-reduce | flops 4096 | bytes 32768 | tf_op jit(solution)/shard_map/pmax | solution.py:98
  329.4 56.1 %psum.22 = f32[4096]{0:T(1024)S(1)} all-reduce(f32[4096]{0:T(1024)S(1)} %exponential_multiply_fusion.1), channel_id=1, replica_groups=mesh['cluster'=8,'row'=16] {'row'}, use_global_device_ids=true, to_apply=%region_21.22 | all-reduce | flops 4096 | bytes 32768 | tf_op jit(solution)/shard_map/psum | solution.py:99
  385.6 12.8 %while.104 = (s32[]{:T(128)}, f32[256]{0:T(256)S(1)}, f32[256]{0:T(256)S(1)}, f32[8,512]{1,0:T(8,128)S(1)}, f32[256]{0:T(256)S(1)}, /*index=5*/f32[8,512]{1,0:T(...) while((s32[]{:T(128)}, f32[256]{0:T(256)S(1)}, ...), condition=%wide.region_25.26_spmd.clone, body=%wide.region_22.25_spmd.clone.sunk | while | flops 135398656 | bytes 1862260 | solution.py:79
  398.4 13.7 %while.101 = (s32[]{:T(128)}, f32[8,512]{1,0:T(8,128)S(1)}, f32[8,512]{1,0:T(8,128)S(1)}, f32[256]{0:T(256)S(1)}, f32[256]{0:T(256)S(1)}, /*index=5*/f32[8,512]{...) while((s32[]{:T(128)}, f32[8,512]{1,0:T(8,128)S(1)}, ...), condition=%wide.region_29.30_spmd, body=%wide.region_26.29_spmd.sunk | while | flops 135396352 | bytes 1858161 | solution.py:95
  412.2 55.6 %pmax.23 = f32[4096]{0:T(1024)S(1)} all-reduce(f32[4096]{0:T(1024)S(1)} %bitcast.274), channel_id=1, replica_groups=mesh['cluster'=8,'row'=16] {'row'}, use_global_device_ids=true, to_apply=%region_30.31 | all-reduce | flops 4096 | bytes 32768 | tf_op jit(solution)/shard_map/pmax | solution.py:98
  467.9 55.6 %psum.23 = f32[4096]{0:T(1024)S(1)} all-reduce(f32[4096]{0:T(1024)S(1)} %exponential_multiply_fusion), channel_id=1, replica_groups=mesh['cluster'=8,'row'=16] {'row'}, use_global_device_ids=true, to_apply=%region_31.32 | all-reduce | flops 4096 | bytes 32768 | tf_op jit(solution)/shard_map/psum | solution.py:99
  523.5 7.0 convolution_convert_fusion
  530.5 12.8 %while.105 = (s32[]{:T(128)}, f32[256]{0:T(256)S(1)}, f32[256]{0:T(256)S(1)}, f32[8,512]{1,0:T(8,128)S(1)}, f32[256]{0:T(256)S(1)}, /*index=5*/f32[8,512]{1,0:T(...) while((s32[]{:T(128)}, f32[256]{0:T(256)S(1)}, ...), condition=%wide.region_35.36_spmd.clone, body=%wide.region_32.35_spmd.clone.sunk | while | flops 135398656 | bytes 1862260 | solution.py:79
  543.4 15.4 %while.106 = (s32[]{:T(128)}, f32[256,512]{1,0:T(8,128)S(1)}, f32[8,512]{1,0:T(8,128)S(1)}, f32[256]{0:T(256)S(1)}, f32[8,512]{1,0:T(8,128)S(1)}, /*index=5*/bf1...) while((s32[]{:T(128)}, f32[256,512]{1,0:T(8,128)S(1)}, ...), condition=%wide.region_37.38_spmd.clone, body=%wide.region_36.37_spmd.clone.sunk | while | flops 269746176 | bytes 2374771 | solution.py:131
  558.8 93.7 %all_to_all.51 = bf16[8,32,512]{2,1,0:T(8,128)(2,1)S(1)} all-to-all(bf16[8,32,512]{2,1,0:T(8,128)(2,1)S(1)} %bitcast.257), channel_id=1, replica_groups=mesh['cluster'=8,'row'=16] {'cluster'}, dimensions={0} | all-to-all | bytes 524288 | tf_op jit(solution)/shard_map/all_to_all | solution.py:138
  652.5 33.7 %reduce-scatter.2.cloned.1.call-done = bf16[256,512]{1,0:T(8,128)(2,1)} async-done(((bf16[4096,512]{1,0:T(8,128)(2,1)}), bf16[256,512]{1,0:T(8,128)(2,1)}) %reduce-scatter.2.cloned.1.call-update) | async-done | bytes 262160 | tf_op jit(solution)/shard_map/reduce_scatter | solution.py:113
  686.3 6.7 all-to-all-start.4
  693.9 5.5 all-to-all-done.4
  (381 shorter events, 116.9 us)
Async XLA Ops:
  7.2 1.0 copy-start
  9.7 12.3 %all-to-all-start.1 = ((bf16[8,32,512]{2,1,0:T(8,128)(2,1)}), bf16[8,32,512]{2,1,0:T(8,128)(2,1)S(1)}, u32[]{:S(2)}, u32[]{:S(2)}) async-start(bf16[8,32,512]{2,1,0:T(8,128)(2,1)} %bitcast.16), calls=%async_computation.1 | async-start | bytes 524288 | tf_op jit(solution)/shard_map/all_to_all | solution.py:51
  34.3 69.4 %all-to-all-start.2 = ((bf16[16,256,512]{2,1,0:T(8,128)(2,1)}), bf16[16,256,512]{2,1,0:T(8,128)(2,1)}, u32[]{:S(2)}, u32[]{:S(2)}) async-start(bf16[16,256,512]{2,1,0:T(8,128)(2,1)} %stack.5), calls=%async_computation.2 | async-start | bytes 8388608 | tf_op jit(solution)/shard_map/all_to_all | solution.py:14
  42.1 644.1 %reduce-scatter.2.cloned.1.call-start = ((), (), s32[]{:S(2)}) async-start(), calls=%async_computation.6 | async-start | bytes 4456448 | tf_op jit(solution)/shard_map/reduce_scatter | solution.py:113
  543.4 149.6 %copy-start.1 = (s32[256]{0:T(256)S(1)}, s32[256]{0:T(256)}, u32[]{:S(2)}) copy-start(s32[256]{0:T(256)} %param.22) | copy-start | bytes 3076
  543.4 156.1 %copy-start.2 = (s32[256]{0:T(256)S(1)}, s32[256]{0:T(256)}, u32[]{:S(2)}) copy-start(s32[256]{0:T(256)} %param.23) | copy-start | bytes 3076
  686.3 13.2 %all-to-all-start.4 = ((bf16[8,32,512]{2,1,0:T(8,128)(2,1)}), bf16[8,32,512]{2,1,0:T(8,128)(2,1)S(1)}, u32[]{:S(2)}, u32[]{:S(2)}) async-start(bf16[8,32,512]{2,1,0:T(8,128)(2,1)} %bitcast.262), calls=%async_computation.5 | async-start | bytes 524288 | tf_op jit(solution)/shard_map/all_to_all | solution.py:139
Sparse Core Ops, SparseCore 0:
  530.6 155.5 reduce-scatter.1
